TPU v7x, 32 devices: a whole 2x2x4 slice. The times are simulated.
32 devices in a mesh: narrow: 4 (over z), wide: 8 (over y, x, core).
Axes of the slice: x: 2, y: 2, z: 4, core: 2. Of those that a mesh axis runs over, the one named last changes fastest.
Arguments:
- layer_input: bfloat16 [32, 512, 640], P(('narrow', 'wide')), may hold values from -6 to 6
- segments: int32 [32, 512], P(('narrow', 'wide')), may hold values from 0 to 7, never falling along the last dimension, each value on 1 to 192 neighbouring positions
- targets: int32 [32, 512], P(('narrow', 'wide')), may hold values from 0 to 24
- loss_mask: int32 [32, 512], P(('narrow', 'wide')), may hold values from 0 to 1
- readout: bfloat16 [640, 25], replicated, may hold values from -0.29882812 to 0.29882812
- attend_gain: bfloat16 [640], P('wide'), may hold values from 0.5 to 1.5
- attend_shift: bfloat16 [640], P('wide'), may hold values from -1.1953125 to 1.1953125
- heads_weight: bfloat16 [640, 1920], P('wide'), may hold values from -0.25 to 0.25
- query_bias: bfloat16 [640], P('wide'), may hold values from -1.1953125 to 1.1953125
- value_bias: bfloat16 [640], P('wide'), may hold values from -1.1953125 to 1.1953125
- output_weight: bfloat16 [640, 640], P('wide'), may hold values from -1.25 to 1.25
- output_bias: bfloat16 [640], P('wide'), may hold values from -1.1953125 to 1.1953125
- forward_gain: bfloat16 [640], P('wide'), may hold values from 0.5 to 1.5
- forward_shift: bfloat16 [640], P('wide'), may hold values from -1.1953125 to 1.1953125
- up_weight: bfloat16 [640, 5120], P('wide'), may hold values from -0.25 to 0.25
- up_bias: bfloat16 [5120], P('wide'), may hold values from -1.1953125 to 1.1953125
- down_weight: bfloat16 [5120, 640], P('wide'), may hold values from -0.125 to 0.125
- down_bias: bfloat16 [640], P('wide'), may hold values from -1.1953125 to 1.1953125
Outputs:
- layer_output: bfloat16 [32, 512, 640], P(('narrow', 'wide'))
- input_grad: float32 [32, 512, 640], P(('narrow', 'wide'))
- attend_gain_grad: float32 [640], P('wide')
- attend_shift_grad: float32 [640], P('wide')
- heads_weight_grad: float32 [640, 1920], P('wide')
- query_bias_grad: float32 [640], P('wide')
- value_bias_grad: float32 [640], P('wide')
- output_weight_grad: float32 [640, 640], P('wide')
- output_bias_grad: float32 [640], P('wide')
- forward_gain_grad: float32 [640], P('wide')
- forward_shift_grad: float32 [640], P('wide')
- up_weight_grad: float32 [640, 5120], P('wide')
- up_bias_grad: float32 [5120], P('wide')
- down_weight_grad: float32 [5120, 640], P('wide')
- down_bias_grad: float32 [640], P('wide')
- loss_sum: float32 [], replicated
- token_count: int32 [], replicated
All inputs are finite; a program needn't handle non-finite values.
Results may differ from a plain program's by a relative error of at most 0.013.
Values may be sent and summed in bfloat16 or wider, within the bound.
No kernel may reach another device: no remote copies, remote signals or barrier semaphores. Data moves between devices by JAX's collectives and lax.ppermute only.
A program may use at most 192 MiB of HBM per device.

v0:
```python
import math
import jax
import jax.numpy as jnp
from jax import lax
from jax.sharding import PartitionSpec as P

HEADS = 20
HEAD_DIM = 32


def normalize(values, gain, shift):
    average = jnp.mean(values, axis=-1, keepdims=True)
    centred = values - average
    spread = jnp.mean(centred * centred, axis=-1, keepdims=True)
    return centred * lax.rsqrt(spread + 1e-05) * gain + shift


def exact_gelu(values):
    return jax.nn.gelu(values, approximate=False)


def masked_scores(query_block, keyset, segment_block, segment_row):
    scale = 1.0 / math.sqrt(HEAD_DIM)
    scores = (
        jnp.einsum("qhd,khd->hqk", query_block, keyset, preferred_element_type=jnp.float32) * scale
    )
    allowed = (segment_block[:, None] == segment_row[None, :])[None]
    return jnp.where(allowed, scores, -1e30)


def local(
    layer_input,
    segments,
    targets,
    loss_mask,
    readout,
    attend_gain,
    attend_shift,
    heads_weight,
    query_bias,
    value_bias,
    output_weight,
    output_bias,
    forward_gain,
    forward_shift,
    up_weight,
    up_bias,
    down_weight,
    down_bias,
):
    length = layer_input.shape[1]
    width = layer_input.shape[2]
    block = min(512, length)
    count_blocks = length // block
    scale = 1.0 / math.sqrt(HEAD_DIM)
    inputs = layer_input[0].astype(jnp.float32)
    segment_row = segments[0]
    attend_set = (
        lax.all_gather(attend_gain, "wide", axis=0, tiled=True),
        lax.all_gather(attend_shift, "wide", axis=0, tiled=True),
        lax.all_gather(heads_weight, "wide", axis=0, tiled=True),
        lax.all_gather(query_bias, "wide", axis=0, tiled=True),
        lax.all_gather(value_bias, "wide", axis=0, tiled=True),
        lax.all_gather(output_weight, "wide", axis=0, tiled=True),
        lax.all_gather(output_bias, "wide", axis=0, tiled=True),
    )
    first_normed, first_pull = jax.vjp(
        normalize, inputs, attend_set[0].astype(jnp.float32), attend_set[1].astype(jnp.float32)
    )
    first_low = first_normed.astype(jnp.bfloat16)
    bias_row = jnp.concatenate(
        [attend_set[3], jnp.zeros_like(attend_set[3]), attend_set[4]]
    ).astype(jnp.float32)
    joined = (
        jnp.dot(first_low, attend_set[2], preferred_element_type=jnp.float32) + bias_row
    ).astype(jnp.bfloat16)
    split_heads = joined.reshape(length, 3, HEADS, HEAD_DIM)
    keyset = split_heads[:, 1]
    valueset = split_heads[:, 2]
    query_blocks = split_heads[:, 0].reshape(count_blocks, block, HEADS, HEAD_DIM)
    segment_blocks = segment_row.reshape(count_blocks, block)

    def forward_block(pieces):
        query_block, segment_block = pieces
        scores = masked_scores(query_block, keyset, segment_block, segment_row)
        highest = jnp.max(scores, axis=-1, keepdims=True)
        shifted = jnp.exp(scores - highest)
        totals = jnp.sum(shifted, axis=-1, keepdims=True)
        probs_low = (shifted / totals).astype(jnp.bfloat16)
        output = jnp.einsum("hqk,khd->qhd", probs_low, valueset, preferred_element_type=jnp.float32)
        return (output.astype(jnp.bfloat16), (highest + jnp.log(totals))[..., 0])

    attended_blocks, lse_blocks = lax.map(forward_block, (query_blocks, segment_blocks))
    attended = attended_blocks.reshape(length, width)
    middle = (
        inputs
        + jnp.dot(attended, attend_set[5], preferred_element_type=jnp.float32)
        + attend_set[6].astype(jnp.float32)
    )
    forward_set = (
        lax.all_gather(forward_gain, "wide", axis=0, tiled=True),
        lax.all_gather(forward_shift, "wide", axis=0, tiled=True),
        lax.all_gather(up_weight, "wide", axis=0, tiled=True),
        lax.all_gather(up_bias, "wide", axis=0, tiled=True),
        lax.all_gather(down_weight, "wide", axis=0, tiled=True),
        lax.all_gather(down_bias, "wide", axis=0, tiled=True),
    )
    second_normed, second_pull = jax.vjp(
        normalize, middle, forward_set[0].astype(jnp.float32), forward_set[1].astype(jnp.float32)
    )
    second_low = second_normed.astype(jnp.bfloat16)
    upward = jnp.dot(second_low, forward_set[2], preferred_element_type=jnp.float32) + forward_set[
        3
    ].astype(jnp.float32)
    activated, gelu_pull = jax.vjp(exact_gelu, upward)
    activated_low = activated.astype(jnp.bfloat16)
    result = (
        middle
        + jnp.dot(activated_low, forward_set[4], preferred_element_type=jnp.float32)
        + forward_set[5].astype(jnp.float32)
    )
    result_low = result.astype(jnp.bfloat16)
    logits = jnp.dot(result_low, readout, preferred_element_type=jnp.float32)
    highest_logit = jnp.max(logits, axis=-1, keepdims=True)
    shifted_logits = jnp.exp(logits - highest_logit)
    logit_totals = jnp.sum(shifted_logits, axis=-1, keepdims=True)
    log_total = highest_logit[:, 0] + jnp.log(logit_totals[:, 0])
    onehot = lax.broadcasted_iota(jnp.int32, logits.shape, 1) == targets[0][:, None]
    picked = jnp.sum(jnp.where(onehot, logits, 0.0), axis=-1)
    weights_row = loss_mask[0].astype(jnp.float32)
    loss_local = jnp.sum((log_total - picked) * weights_row)
    count_local = jnp.sum(weights_row)
    wide_count = lax.axis_size("wide")
    loss_column = jnp.full((wide_count,), loss_local)
    count_column = jnp.full((wide_count,), count_local)
    grad_logits = (
        weights_row[:, None] * (shifted_logits / logit_totals - onehot.astype(jnp.float32))
    ).astype(jnp.bfloat16)
    grad_result = jnp.einsum("lv,dv->ld", grad_logits, readout, preferred_element_type=jnp.float32)
    up_matrix, down_matrix = (
        lax.all_gather(up_weight, "wide", axis=0, tiled=True),
        lax.all_gather(down_weight, "wide", axis=0, tiled=True),
    )
    grad_down = grad_result.astype(jnp.bfloat16)
    down_weight_part = jnp.einsum(
        "lf,ld->fd", activated_low, grad_down, preferred_element_type=jnp.float32
    )
    down_bias_part = jnp.sum(grad_down, axis=0, dtype=jnp.float32)
    grad_activated = jnp.einsum(
        "ld,fd->lf", grad_down, down_matrix, preferred_element_type=jnp.float32
    )
    grad_up = gelu_pull(grad_activated)[0].astype(jnp.bfloat16)
    up_weight_part = jnp.einsum(
        "ld,lf->df", second_low, grad_up, preferred_element_type=jnp.float32
    )
    up_bias_part = jnp.sum(grad_up, axis=0, dtype=jnp.float32)
    grad_second = jnp.einsum("lf,df->ld", grad_up, up_matrix, preferred_element_type=jnp.float32)
    middle_part, forward_gain_part, forward_shift_part = second_pull(grad_second)
    grad_middle = grad_result + middle_part
    forward_shards = (
        lax.psum_scatter(forward_gain_part, "wide", scatter_dimension=0, tiled=True),
        lax.psum_scatter(forward_shift_part, "wide", scatter_dimension=0, tiled=True),
        lax.psum_scatter(up_weight_part, "wide", scatter_dimension=0, tiled=True),
        lax.psum_scatter(up_bias_part, "wide", scatter_dimension=0, tiled=True),
        lax.psum_scatter(down_weight_part, "wide", scatter_dimension=0, tiled=True),
        lax.psum_scatter(down_bias_part, "wide", scatter_dimension=0, tiled=True),
        lax.psum_scatter(loss_column, "wide", scatter_dimension=0, tiled=True),
        lax.psum_scatter(count_column, "wide", scatter_dimension=0, tiled=True),
    )
    heads_matrix, output_matrix = (
        lax.all_gather(heads_weight, "wide", axis=0, tiled=True),
        lax.all_gather(output_weight, "wide", axis=0, tiled=True),
    )
    grad_branch = grad_middle.astype(jnp.bfloat16)
    output_weight_part = jnp.einsum(
        "ld,le->de", attended, grad_branch, preferred_element_type=jnp.float32
    )
    output_bias_part = jnp.sum(grad_branch, axis=0, dtype=jnp.float32)
    grad_attended = jnp.einsum(
        "le,de->ld", grad_branch, output_matrix, preferred_element_type=jnp.float32
    ).astype(jnp.bfloat16)
    grad_blocks = grad_attended.reshape(count_blocks, block, HEADS, HEAD_DIM)

    def backward_block(carry, pieces):
        key_sum, value_sum = carry
        query_block, segment_block, grad_block, lse_block = pieces
        scores = masked_scores(query_block, keyset, segment_block, segment_row)
        probs = jnp.exp(scores - lse_block[..., None])
        value_sum = value_sum + jnp.einsum(
            "hqk,qhd->khd",
            probs.astype(jnp.bfloat16),
            grad_block,
            preferred_element_type=jnp.float32,
        )
        grad_probs = jnp.einsum(
            "qhd,khd->hqk", grad_block, valueset, preferred_element_type=jnp.float32
        )
        inner = jnp.sum(probs * grad_probs, axis=-1, keepdims=True)
        grad_scores = (probs * (grad_probs - inner)).astype(jnp.bfloat16)
        grad_query = (
            jnp.einsum("hqk,khd->qhd", grad_scores, keyset, preferred_element_type=jnp.float32)
            * scale
        )
        key_sum = (
            key_sum
            + jnp.einsum(
                "hqk,qhd->khd", grad_scores, query_block, preferred_element_type=jnp.float32
            )
            * scale
        )
        return ((key_sum, value_sum), grad_query)

    zero_heads = jnp.zeros((length, HEADS, HEAD_DIM), jnp.float32)
    (key_sum, value_sum), query_grads = lax.scan(
        backward_block,
        (zero_heads, zero_heads),
        (query_blocks, segment_blocks, grad_blocks, lse_blocks),
    )
    grad_joined = jnp.concatenate(
        [
            query_grads.reshape(length, width),
            key_sum.reshape(length, width),
            value_sum.reshape(length, width),
        ],
        axis=1,
    ).astype(jnp.bfloat16)
    heads_weight_part = jnp.einsum(
        "ld,le->de", first_low, grad_joined, preferred_element_type=jnp.float32
    )
    query_bias_part = jnp.sum(grad_joined[:, :width], axis=0, dtype=jnp.float32)
    value_bias_part = jnp.sum(grad_joined[:, 2 * width :], axis=0, dtype=jnp.float32)
    grad_first = jnp.einsum(
        "le,de->ld", grad_joined, heads_matrix, preferred_element_type=jnp.float32
    )
    input_part, attend_gain_part, attend_shift_part = first_pull(grad_first)
    input_grad = grad_middle + input_part
    attend_shards = (
        lax.psum_scatter(attend_gain_part, "wide", scatter_dimension=0, tiled=True),
        lax.psum_scatter(attend_shift_part, "wide", scatter_dimension=0, tiled=True),
        lax.psum_scatter(heads_weight_part, "wide", scatter_dimension=0, tiled=True),
        lax.psum_scatter(query_bias_part, "wide", scatter_dimension=0, tiled=True),
        lax.psum_scatter(value_bias_part, "wide", scatter_dimension=0, tiled=True),
        lax.psum_scatter(output_weight_part, "wide", scatter_dimension=0, tiled=True),
        lax.psum_scatter(output_bias_part, "wide", scatter_dimension=0, tiled=True),
    )
    summed = (
        lax.psum(attend_shards[0].astype(jnp.bfloat16), "narrow").astype(jnp.float32),
        lax.psum(attend_shards[1].astype(jnp.bfloat16), "narrow").astype(jnp.float32),
        lax.psum(attend_shards[2].astype(jnp.bfloat16), "narrow").astype(jnp.float32),
        lax.psum(attend_shards[3].astype(jnp.bfloat16), "narrow").astype(jnp.float32),
        lax.psum(attend_shards[4].astype(jnp.bfloat16), "narrow").astype(jnp.float32),
        lax.psum(attend_shards[5].astype(jnp.bfloat16), "narrow").astype(jnp.float32),
        lax.psum(attend_shards[6].astype(jnp.bfloat16), "narrow").astype(jnp.float32),
        lax.psum(forward_shards[0].astype(jnp.bfloat16), "narrow").astype(jnp.float32),
        lax.psum(forward_shards[1].astype(jnp.bfloat16), "narrow").astype(jnp.float32),
        lax.psum(forward_shards[2].astype(jnp.bfloat16), "narrow").astype(jnp.float32),
        lax.psum(forward_shards[3].astype(jnp.bfloat16), "narrow").astype(jnp.float32),
        lax.psum(forward_shards[4].astype(jnp.bfloat16), "narrow").astype(jnp.float32),
        lax.psum(forward_shards[5].astype(jnp.bfloat16), "narrow").astype(jnp.float32),
        lax.psum(forward_shards[6].astype(jnp.bfloat16), "narrow").astype(jnp.float32),
        lax.psum(forward_shards[7].astype(jnp.bfloat16), "narrow").astype(jnp.float32),
    )
    loss_total = summed[13][0]
    count_total = summed[14][0]
    return (
        result_low[None],
        input_grad[None],
        summed[0],
        summed[1],
        summed[2],
        summed[3],
        summed[4],
        summed[5],
        summed[6],
        summed[7],
        summed[8],
        summed[9],
        summed[10],
        summed[11],
        summed[12],
        loss_total,
        count_total.astype(jnp.int32),
    )


def solution(mesh):
    in_specs = (
        P(("narrow", "wide"), None, None),
        P(("narrow", "wide"), None),
        P(("narrow", "wide"), None),
        P(("narrow", "wide"), None),
        P(),
        P("wide"),
        P("wide"),
        P("wide", None),
        P("wide"),
        P("wide"),
        P("wide", None),
        P("wide"),
        P("wide"),
        P("wide"),
        P("wide", None),
        P("wide"),
        P("wide", None),
        P("wide"),
    )
    out_specs = (
        P(("narrow", "wide"), None, None),
        P(("narrow", "wide"), None, None),
        P("wide"),
        P("wide"),
        P("wide", None),
        P("wide"),
        P("wide"),
        P("wide", None),
        P("wide"),
        P("wide"),
        P("wide"),
        P("wide", None),
        P("wide"),
        P("wide", None),
        P("wide"),
        P(),
        P(),
    )
    return jax.shard_map(local, mesh=mesh, in_specs=in_specs, out_specs=out_specs, check_vma=False)
```

profile of v0, /device:TPU:0, one launch (start us, length us, event | category | flops | bytes accessed | tf_op | source)
XLA Modules:
  0.0 585.1 jit_solution(7206739429165697035)
XLA Ops:
  22.8 26.0 %all-reduce.20 = (bf16[640]{0:T(1024)(128)(2,1)S(1)}, bf16[640]{0:T(1024)(128)(2,1)S(1)}, bf16[640]{0:T(1024)(128)(2,1)S(1)}, bf16[640]{0:T(1024)(128)(2,1)S(1)}...) all-reduce(bf16[640]{0:T(1024)(128)(2,1)S(1)} %dynamic-update-slice, ...), channel_id=1, replica_groups=mesh['narrow'=4,'wide'=8] {'wide'}, use_global_device_ids=true, to_apply=%add.3 | all-reduce | flops 5120 | bytes 20480
  48.9 8.2 %all-gather = bf16[8,1,640]{2,1,0:T(2,128)(2,1)S(1)} all-gather(bf16[1,1,640]{2,1,0:T(2,128)(2,1)S(1)} %reshape.230), channel_id=1, replica_groups=mesh['narrow'=4,'wide'=8] {'wide'}, dimensions={0}, use_global_device_ids=true | all-gather | bytes 11520 | tf_op jit(solution)/shard_map/all_gather | solution.py:104
  58.1 12.7 %all_gather.48 = bf16[640,640]{1,0:T(8,128)(2,1)} all-gather(bf16[80,640]{1,0:T(8,128)(2,1)} %param.28), channel_id=1, replica_groups=mesh['narrow'=4,'wide'=8] {'wide'}, dimensions={0}, use_global_device_ids=true | all-gather | bytes 921600 | tf_op jit(solution)/shard_map/all_gather | solution.py:64
  70.8 5.1 add_convert_fusion.1
  85.3 4.1 copy-done.2
  89.4 3.9 fusion.28
  94.7 31.0 %multiply_convert_fusion.1 = (bf16[512,5120]{1,0:T(8,128)(2,1)}, f32[512,5120]{1,0:T(8,128)}, f32[512,5120]{1,0:T(8,128)}) fusion(f32[5120]{0:T(1024)S(1)} %bitcast.122, bf16[640,5120]{1,0:T(8,128)(2,1)} %all-gather.7.cloned.1.call-done, f32[512,640]{1,0:T(8,128)S(1)} %get-tuple-element.124, f32[640]{0:T(1024)S(1)} %convert_element_type.218, ...), kind=kOutput, calls=%fused_computation.14 | convolution fusion | flops 3530096640 | bytes 34108416 | tf_op jit(solution)/shard_map/dot_general | solution.py:112
  125.8 13.2 %all-gather.9.cloned.1.call-done = bf16[5120,640]{1,0:T(8,128)(2,1)} async-done(((bf16[640,640]{1,0:T(8,128)(2,1)}), bf16[5120,640]{1,0:T(8,128)(2,1)}) %all-gather.9.cloned.1.call-update) | async-done | bytes 6553616 | tf_op jit(solution)/shard_map/all_gather | solution.py:105
  139.0 8.7 %fusion.24 = bf16[512,640]{1,0:T(8,128)(2,1)S(1)} fusion(f32[512,640]{1,0:T(8,128)S(1)} %get-tuple-element.124, bf16[512,5120]{1,0:T(8,128)(2,1)} %get-tuple-element.115, bf16[5120,640]{1,0:T(8,128)(2,1)} %all-gather.9.cloned.1.call-done, f32[640]{0:T(1024)S(1)} %convert_element_type.222), kind=kOutput, calls=%fused_computation.50 | convolution fusion | flops 3356426240 | bytes 13765120 | tf_op jit(solution)/shard_map/dot_general | solution.py:119
  148.5 14.6 %convert_reduce_fusion = (f32[5120]{0:T(1024)S(1)}, bf16[512,5120]{1,0:T(8,128)(2,1)}) fusion(f32[512,5120]{1,0:T(8,128)} %get-tuple-element.116, bf16[5120,640]{1,0:T(8,128)(2,1)} %all-gather.9.cloned.1.call-done, f32[512,640]{1,0:T(8,128)S(1)} %fusion.39, f32[512,5120]{1,0:T(8,128)} %get-tuple-element.125, f32[5120]{0:T(1024)S(1)} %bitcast.123), kind=kOutput, calls=%fused_computation.11 | convolution fusion | flops 3400330240 | bytes 34119680 | tf_op jit(solution)/shard_map/ld,fd->lf/dot_general | solution.py:149
  163.1 8.5 %multiply_reduce_fusion.1 = (f32[640]{0:T(1024)S(1)}, f32[512]{0:T(512)S(1)}, f32[640]{0:T(1024)S(1)}, f32[512,640]{1,0:T(8,128)S(1)}) fusion(f32[512,640]{1,0:T(8,128)S(1)} %copy-done.4, f32[512]{0:T(512)S(1)} %fusion.45, f32[512]{0:T(512)S(1)} %broadcast_multiply_fusion, f32[640]{0:T(1024)S(1)} %convert_element_type.217, ...), kind=kOutput, calls=%fused_computation.60 | convolution fusion | flops 3358063104 | bytes 14431744 | tf_op jit(solution)/shard_map/lf,df->ld/dot_general | solution.py:157
  179.3 13.9 %multiply_reduce_fusion = (f32[20,512]{1,0:T(8,128)S(1)}, f32[20,512,512]{1,2,0:T(8,128)}) fusion(f32[20,512,512]{1,2,0:T(8,128)} %copy-done.2, f32[20,512]{1,0:T(8,128)S(1)} %log_add_fusion, bf16[512,20,32]{0,2,1:T(8,128)(2,1)} %bitcast.111, bf16[512,3,20,32]{0,3,2,1:T(8,128)(2,1)S(1)} %bitcast.108), kind=kOutput, calls=%fused_computation.1 | convolution fusion | flops 351262720 | bytes 43343872 | tf_op jit(solution)/shard_map/while/body/eval_jaxpr/qhd,khd->hqk/dot_general | solution.py:195
  193.2 14.9 %multiply_convert_fusion = bf16[20,512,512]{1,2,0:T(8,128)(2,1)S(1)} fusion(f32[20,512,512]{1,2,0:T(8,128)} %get-tuple-element.130, f32[20,512,512]{1,2,0:T(8,128)} %copy-done.2, f32[20,512]{1,0:T(8,128)S(1)} %get-tuple-element.129, f32[20,512]{1,0:T(8,128)S(1)} %log_add_fusion), kind=kLoop, calls=%fused_computation | loop fusion | flops 20971520 | bytes 52510720 | tf_op jit(solution)/shard_map/while/body/eval_jaxpr/convert_element_type | solution.py:199
  212.9 9.1 %fusion.25 = bf16[20,32,512]{2,1,0:T(8,128)(2,1)S(1)} fusion(bf16[512,20,32]{0,2,1:T(8,128)(2,1)S(1)} %bitcast.112, f32[20,512,512]{1,2,0:T(8,128)} %copy-done.2, f32[20,512]{1,0:T(8,128)S(1)} %log_add_fusion), kind=kOutput, calls=%fused_computation.51 | convolution fusion | flops 346357760 | bytes 22323200 | tf_op jit(solution)/shard_map/while/body/eval_jaxpr/hqk,qhd->khd/dot_general | solution.py:189
  222.8 4.1 fusion.34
  228.3 12.3 %fusion.57 = f32[640,5120]{1,0:T(8,128)} fusion(bf16[512,5120]{1,0:T(8,128)(2,1)} %get-tuple-element.133, f32[512,640]{1,0:T(8,128)S(1)} %copy-done.5, f32[640]{0:T(1024)S(1)} %convert_element_type.218, f32[640]{0:T(1024)S(1)} %convert_element_type.217, f32[512]{0:T(512)S(1)} %fusion.45, f32[512]{0:T(512)S(1)} %broadcast_multiply_fusion), kind=kOutput, calls=%fused_computation.117 | convolution fusion | flops 3357081600 | bytes 19670016 | tf_op jit(solution)/shard_map/ld,lf->df/dot_general | solution.py:153
  240.6 12.1 %fusion.48 = f32[5120,640]{1,0:T(8,128)} fusion(bf16[512,5120]{1,0:T(8,128)(2,1)} %get-tuple-element.115, f32[512,640]{1,0:T(8,128)S(1)} %fusion.39), kind=kOutput, calls=%fused_computation.111 | convolution fusion | flops 3355770880 | bytes 19660800 | tf_op jit(solution)/shard_map/lf,ld->fd/dot_general | solution.py:145
  254.7 27.3 %reduce-scatter.5.cloned.1.call-done = f32[80,1920]{1,0:T(8,128)} async-done(((f32[640,1920]{1,0:T(8,128)}), f32[80,1920]{1,0:T(8,128)}) %reduce-scatter.5.cloned.1.call-update) | async-done | bytes 614416 | tf_op jit(solution)/shard_map/reduce_scatter | solution.py:240
  283.9 96.4 %reduce-scatter.9.cloned.1.call-done = f32[80,5120]{1,0:T(8,128)} async-done(((f32[640,5120]{1,0:T(8,128)}), f32[80,5120]{1,0:T(8,128)}) %reduce-scatter.9.cloned.1.call-update) | async-done | bytes 1638416 | tf_op jit(solution)/shard_map/reduce_scatter | solution.py:163
  382.7 95.9 %reduce-scatter.11.cloned.1.call-done = f32[640,640]{1,0:T(8,128)} async-done(((f32[5120,640]{1,0:T(8,128)}), f32[640,640]{1,0:T(8,128)}) %reduce-scatter.11.cloned.1.call-update) | async-done | bytes 1638416 | tf_op jit(solution)/shard_map/reduce_scatter | solution.py:165
  483.9 4.0 fusion.59
  491.6 25.0 %all-reduce.19 = (bf16[640]{0:T(1024)(128)(2,1)S(1)}, bf16[640]{0:T(1024)(128)(2,1)S(1)}, bf16[640]{0:T(1024)(128)(2,1)S(1)}, bf16[640]{0:T(1024)(128)(2,1)S(1)}...) all-reduce(f32[640]{0:T(1024)S(1)} %get-tuple-element.70, ...), channel_id=2, replica_groups=mesh['narrow'=4,'wide'=8] {'wide'}, use_global_device_ids=true, to_apply=%region_14.15.clone | all-reduce | flops 10256 | bytes 61536
  519.8 12.4 %all-reduce.21 = (bf16[80]{0:T(256)(128)(2,1)S(1)}, bf16[80]{0:T(256)(128)(2,1)S(1)}, bf16[80]{0:T(256)(128)(2,1)S(1)}, bf16[80]{0:T(256)(128)(2,1)S(1)}, bf16[8...) all-reduce(bf16[80]{0:T(256)(128)(2,1)S(1)} %dynamic-slice.47, ...), channel_id=1, replica_groups=mesh['narrow'=4,'wide'=8] {'narrow'}, use_global_device_ids=true, to_apply=%region_15.16 | all-reduce | flops 1282 | bytes 5128 | tf_op jit(solution)/shard_map/psum | solution.py:247
  538.2 29.3 %all-reduce.25.cloned.1.call-done = (bf16[80,1920]{1,0:T(8,128)(2,1)}, bf16[80,640]{1,0:T(8,128)(2,1)}, bf16[80,5120]{1,0:T(8,128)(2,1)}, bf16[640,640]{1,0:T(8,128)(2,1)}) async-done(((bf16[80,1920]{1,0:T(8,128)(2,1)}, bf16[80,640]{1,0:T(8,128)(2,1)}, bf16[80,5120]{1,0:T(8,128)(2,1)}, bf16[640,640]{1,0:T(8,128)(2,1)}), (bf16[80,1920]{1,0:T(8,128)(2,1)}, bf16[80,640]{1,0:T(8,128)(2,1)}, ...) | async-done | bytes 2048016 | tf_op jit(solution)/shard_map/psum | solution.py:249
  (174 shorter events, 71.8 us)
Async XLA Ops:
  7.2 140.5 %copy-start = (bf16[640,25]{0,1:T(8,128)(2,1)S(1)}, bf16[640,25]{0,1:T(8,128)(2,1)}, u32[]{:S(2)}) copy-start(bf16[640,25]{0,1:T(8,128)(2,1)} %param.22) | copy-start | bytes 96004
  7.2 63.6 %all-gather.5.cloned.1.call-start = ((), (), s32[]{:S(2)}) async-start(), calls=%async_computation.4 | async-start | bytes 2764800 | tf_op jit(solution)/shard_map/all_gather | solution.py:61
  7.9 86.8 %all-gather.7.cloned.1.call-start = ((), (), s32[]{:S(2)}) async-start(), calls=%async_computation.5 | async-start | bytes 7372800 | tf_op jit(solution)/shard_map/all_gather | solution.py:103
  8.7 130.3 %all-gather.9.cloned.1.call-start = ((), (), s32[]{:S(2)}) async-start(), calls=%async_computation.6 | async-start | bytes 7372800 | tf_op jit(solution)/shard_map/all_gather | solution.py:105
  9.4 243.6 %reduce-scatter.7.cloned.1.call-start = ((), (), s32[]{:S(2)}) async-start(), calls=%async_computation.8 | async-start | bytes 1843200 | tf_op jit(solution)/shard_map/reduce_scatter | solution.py:243
  11.4 64.5 %copy-start.23 = (f32[512]{0:T(512)}, f32[512]{0:T(512)S(1)}, u32[]{:S(2)}) copy-start(f32[512]{0:T(512)S(1)} %broadcast_multiply_fusion.1) | copy-start | bytes 6148
  13.4 62.5 %copy-start.27 = (f32[512]{0:T(512)}, f32[512]{0:T(512)S(1)}, u32[]{:S(2)}) copy-start(f32[512]{0:T(512)S(1)} %fusion.44) | copy-start | bytes 6148
  48.8 27.1 %copy-start.21 = (f32[640]{0:T(1024)}, f32[640]{0:T(1024)S(1)}, u32[]{:S(2)}) copy-start(f32[640]{0:T(1024)S(1)} %convert_element_type.208) | copy-start | bytes 7684
  48.8 27.1 %copy-start.31 = (f32[640]{0:T(1024)}, f32[640]{0:T(1024)S(1)}, u32[]{:S(2)}) copy-start(f32[640]{0:T(1024)S(1)} %convert_element_type.209) | copy-start | bytes 7684
  94.3 44.7 %copy-start.3 = (f32[512,640]{1,0:T(8,128)}, f32[512,640]{1,0:T(8,128)S(1)}, u32[]{:S(2)}) copy-start(f32[512,640]{1,0:T(8,128)S(1)} %get-tuple-element.124) | copy-start | bytes 3932164
  148.5 14.6 %copy-start.4 = (f32[512,640]{1,0:T(8,128)S(1)}, f32[512,640]{1,0:T(8,128)}, u32[]{:S(2)}) copy-start(f32[512,640]{1,0:T(8,128)} %copy-done.3) | copy-start | bytes 3932164
  179.3 102.8 %reduce-scatter.5.cloned.1.call-start = ((), (), s32[]{:S(2)}) async-start(), calls=%async_computation.7 | async-start | bytes 5529600 | tf_op jit(solution)/shard_map/reduce_scatter | solution.py:240
  209.6 12.4 %copy-start.11 = (bf16[20,32,512]{2,1,0:T(8,128)(2,1)}, bf16[20,32,512]{2,1,0:T(8,128)(2,1)S(1)}, u32[]{:S(2)}) copy-start(bf16[20,32,512]{2,1,0:T(8,128)(2,1)S(1)} %fusion.22) | copy-start | bytes 1966084
  212.8 10.0 %copy-start.9 = (bf16[1,512,640]{2,1,0:T(8,128)(2,1)S(1)}, bf16[1,512,640]{2,1,0:T(8,128)(2,1)}, u32[]{:S(2)}) copy-start(bf16[1,512,640]{2,1,0:T(8,128)(2,1)} %param.18) | copy-start | bytes 1966084
  212.8 10.0 %copy-start.22 = (f32[640]{0:T(1024)S(1)}, f32[640]{0:T(1024)}, u32[]{:S(2)}) copy-start(f32[640]{0:T(1024)} %copy-done.21) | copy-start | bytes 7684
  212.8 10.0 %copy-start.24 = (f32[512]{0:T(512)S(1)}, f32[512]{0:T(512)}, u32[]{:S(2)}) copy-start(f32[512]{0:T(512)} %copy-done.23) | copy-start | bytes 6148
  212.8 10.0 %copy-start.28 = (f32[512]{0:T(512)S(1)}, f32[512]{0:T(512)}, u32[]{:S(2)}) copy-start(f32[512]{0:T(512)} %copy-done.27) | copy-start | bytes 6148
  227.0 153.3 %reduce-scatter.9.cloned.1.call-start = ((), (), s32[]{:S(2)}) async-start(), calls=%async_computation.9 | async-start | bytes 14745600 | tf_op jit(solution)/shard_map/reduce_scatter | solution.py:163
  240.5 238.0 %reduce-scatter.11.cloned.1.call-start = ((), (), s32[]{:S(2)}) async-start(), calls=%async_computation.10 | async-start | bytes 14745600 | tf_op jit(solution)/shard_map/reduce_scatter | solution.py:165
  252.7 229.6 %copy-start.30 = (s32[1,512]{1,0:T(1,128)S(1)}, s32[1,512]{1,0:T(1,128)}, u32[]{:S(2)}) copy-start(s32[1,512]{1,0:T(1,128)} %param.21) | copy-start | bytes 6148
  252.7 230.8 %copy-start.12 = (bf16[20,32,512]{2,1,0:T(8,128)(2,1)S(1)}, bf16[20,32,512]{2,1,0:T(8,128)(2,1)}, u32[]{:S(2)}) copy-start(bf16[20,32,512]{2,1,0:T(8,128)(2,1)} %copy-done.11) | copy-start | bytes 1966084
  252.7 230.8 %copy-start.14 = (bf16[20,32,512]{2,1,0:T(8,128)(2,1)S(1)}, bf16[20,32,512]{2,1,0:T(8,128)(2,1)}, u32[]{:S(2)}) copy-start(bf16[20,32,512]{2,1,0:T(8,128)(2,1)} %copy-done.13) | copy-start | bytes 1966084
  252.8 314.8 %all-reduce.25.cloned.1.call-start = ((), (), s32[]{:S(2)}) async-start(), calls=%async_computation.11 | async-start | bytes 4096000 | tf_op jit(solution)/shard_map/psum | solution.py:249
  488.6 87.2 %copy-start.1 = (bf16[640,25]{0,1:T(8,128)(2,1)S(1)}, bf16[640,25]{0,1:T(8,128)(2,1)}, u32[]{:S(2)}) copy-start(bf16[640,25]{0,1:T(8,128)(2,1)} %param.22) | copy-start | bytes 96004
  (17 other events, 66.8 us)
Sparse Core Ops, SparseCore 0:
  9.9 32.1 all-gather.4
  44.0 46.4 all-gather.6
  92.4 46.5 all-gather.8
  179.4 38.6 reduce-scatter.6
  227.1 54.9 reduce-scatter.4
  285.5 94.6 reduce-scatter.8
  383.8 94.6 reduce-scatter.10
  482.4 85.1 all-reduce.24
where the time goes:
time: 589 us; the launch traced here: 585 us
  waiting for transfers between devices  264 us (45%)
  matrix products  141 us (24%)
  blocking collectives  84.4 us (14%)
  other arithmetic  48.7 us (8%)
  local copies, waits for them, and re-layouts  25.6 us (4%)
  between operations  20.5 us (3%)
    reduce_scatter x1, waiting for transfers between devices, local(): lax.psum_scatter(up_weight_part, 'wide', scatter_dimension=0, tiled=True)  96.4 us
    reduce_scatter x1, waiting for transfers between devices, local(): lax.psum_scatter(down_weight_part, 'wide', scatter_dimension=0, tiled=True)  95.9 us
    unnamed x2, blocking collectives  51 us
    dot_general x1, matrix products, local(): jnp.dot(second_low, forward_set[2], preferred_element_type=jnp.float32)  31 us
    psum x1, waiting for transfers between devices, local(): lax.psum(attend_shards[2].astype(jnp.bfloat16), 'narrow')  29.3 us
    reduce_scatter x1, waiting for transfers between devices, local(): lax.psum_scatter(heads_weight_part, 'wide', scatter_dimension=0, tiled=True)  27.3 us
    unnamed x96, local copies, waits for them, and re-layouts  19.4 us
    convert_element_type x1, other arithmetic, backward_block(): grad_scores = (probs * (grad_probs - inner)).astype(jnp.bfloat16)  14.9 us
  transfers between devices with their start and end apart: 8, of which 5 were waited for; matrix products, arithmetic and copies ran while one was open for 27% of the time, Pallas kernels for 0%

commit v1 on v0

--- a/solution.py
+++ b/solution.py
@@ -97,12 +97,26 @@
         + jnp.dot(attended, attend_set[5], preferred_element_type=jnp.float32)
         + attend_set[6].astype(jnp.float32)
     )
+
+    def update_scenes(local_values):
+        last = jax.lax.axis_index("wide")
+        later = jax.lax.axis_size("wide")
+        d_next, outcome_arr = (later, last)
+        z_new, plain = (local_values, 1)
+        while plain < d_next:
+            new = jax.lax.ppermute(z_new, "wide", [(it, it ^ plain) for it in range(d_next)])
+            all_values = jnp.concatenate([z_new, new], 0)
+            f_now = jnp.concatenate([new, z_new], axis=0)
+            z_new = jnp.where(outcome_arr & plain == 0, all_values, f_now)
+            plain = 2 * plain
+        return z_new
+
     forward_set = (
         lax.all_gather(forward_gain, "wide", axis=0, tiled=True),
         lax.all_gather(forward_shift, "wide", axis=0, tiled=True),
         lax.all_gather(up_weight, "wide", axis=0, tiled=True),
         lax.all_gather(up_bias, "wide", axis=0, tiled=True),
-        lax.all_gather(down_weight, "wide", axis=0, tiled=True),
+        update_scenes(down_weight),
         lax.all_gather(down_bias, "wide", axis=0, tiled=True),
     )
     second_normed, second_pull = jax.vjp(

time: 589 us -> 661 us (1.12)
  blocking collectives: 84.4 us -> 122 us
  waiting for transfers between devices: 264 us -> 297 us
    ppermute x0 -> x3, waiting for transfers between devices: none -> 46.6 us  [update_scenes(): jax.lax.ppermute(z_new, 'wide', [(it, it ^ plain) for it in range(d_next)])]
    unnamed x2, blocking collectives: 51 us -> 87.5 us
    all_gather x1, waiting for transfers between devices: 13.2 us -> 0.02 us  [local(): lax.all_gather(down_weight, 'wide', axis=0, tiled=True)]
    select_n x0 -> x2, other arithmetic: none -> 6.66 us  [update_scenes(): z_new = jnp.where(outcome_arr & plain == 0, all_values, f_now)]
    unnamed x96 -> x130, local copies, waits for them, and re-layouts: 19.4 us -> 13.1 us
  transfers between devices with their start and end apart: 8 -> 11, of which waited for: 5 -> 6; matrix products, arithmetic and copies ran while one was open for 27% -> 25% of each run, Pallas kernels for 0% -> 0%
where the time goes in v1:
time: 661 us; the launch traced here: 657 us
  waiting for transfers between devices  297 us (45%)
  matrix products  141 us (21%)
  blocking collectives  122 us (18%)
  other arithmetic  51.3 us (8%)
  between operations  20.8 us (3%)
  local copies, waits for them, and re-layouts  19.3 us (3%)
    reduce_scatter x1, waiting for transfers between devices, local(): lax.psum_scatter(up_weight_part, 'wide', scatter_dimension=0, tiled=True)  96.4 us
    reduce_scatter x1, waiting for transfers between devices, local(): lax.psum_scatter(down_weight_part, 'wide', scatter_dimension=0, tiled=True)  95.9 us
    unnamed x2, blocking collectives  87.5 us
    ppermute x3, waiting for transfers between devices, update_scenes(): jax.lax.ppermute(z_new, 'wide', [(it, it ^ plain) for it in range(d_next)])  46.6 us
    dot_general x1, matrix products, local(): jnp.dot(second_low, forward_set[2], preferred_element_type=jnp.float32)  30.6 us
    psum x1, waiting for transfers between devices, local(): lax.psum(attend_shards[2].astype(jnp.bfloat16), 'narrow')  29.3 us
    reduce_scatter x1, waiting for transfers between devices, local(): lax.psum_scatter(heads_weight_part, 'wide', scatter_dimension=0, tiled=True)  27.5 us
    convert_element_type x1, other arithmetic, backward_block(): grad_scores = (probs * (grad_probs - inner)).astype(jnp.bfloat16)  14.9 us
  transfers between devices with their start and end apart: 11, of which 6 were waited for; matrix products, arithmetic and copies ran while one was open for 25% of the time, Pallas kernels for 0%

profile of v1, /device:TPU:0, one launch (start us, length us, event | category | flops | bytes accessed | tf_op | source)
XLA Modules:
  0.0 657.0 jit_solution(14458966337452110803)
XLA Ops:
  19.8 62.5 %all-reduce.20 = (bf16[640]{0:T(1024)(128)(2,1)S(1)}, bf16[640]{0:T(1024)(128)(2,1)S(1)}, bf16[640]{0:T(1024)(128)(2,1)S(1)}, bf16[640]{0:T(1024)(128)(2,1)S(1)}...) all-reduce(bf16[640]{0:T(1024)(128)(2,1)S(1)} %dynamic-update-slice, ...), channel_id=1, replica_groups=mesh['narrow'=4,'wide'=8] {'wide'}, use_global_device_ids=true, to_apply=%add.3 | all-reduce | flops 5120 | bytes 20480
  82.4 9.5 %all-gather = bf16[8,1,640]{2,1,0:T(2,128)(2,1)S(1)} all-gather(bf16[1,1,640]{2,1,0:T(2,128)(2,1)S(1)} %reshape.230), channel_id=1, replica_groups=mesh['narrow'=4,'wide'=8] {'wide'}, dimensions={0}, use_global_device_ids=true | all-gather | bytes 11520 | tf_op jit(solution)/shard_map/all_gather | solution.py:118
  92.5 12.8 %all_gather.47 = bf16[640,640]{1,0:T(8,128)(2,1)} all-gather(bf16[80,640]{1,0:T(8,128)(2,1)S(1)} %copy-done.25), channel_id=1, replica_groups=mesh['narrow'=4,'wide'=8] {'wide'}, dimensions={0}, use_global_device_ids=true | all-gather | bytes 921600 | tf_op jit(solution)/shard_map/all_gather | solution.py:64
  106.2 4.7 maximum_select_fusion.2
  111.9 5.1 add_convert_fusion.1
  130.4 3.9 fusion.36
  135.7 30.6 %multiply_convert_fusion.1 = (bf16[512,5120]{1,0:T(8,128)(2,1)S(1)}, f32[512,5120]{1,0:T(8,128)}, f32[512,5120]{1,0:T(8,128)}) fusion(f32[5120]{0:T(1024)S(1)} %bitcast.121, bf16[640,5120]{1,0:T(8,128)(2,1)} %all-gather.7.cloned.1.call-done, f32[512,640]{1,0:T(8,128)S(1)} %get-tuple-element.124, f32[640]{0:T(1024)S(1)} %convert_element_type.218, ...), kind=kOutput, calls=%fused_computation.14 | convolution fusion | flops 3530096640 | bytes 34108416 | tf_op jit(solution)/shard_map/dot_general | solution.py:126
  166.3 44.4 %collective-permute-done.2 = bf16[2560,640]{1,0:T(8,128)(2,1)} collective-permute-done((bf16[2560,640]{1,0:T(8,128)(2,1)}, bf16[2560,640]{1,0:T(8,128)(2,1)}, u32[]{:S(2)}, u32[]{:S(2)}) %collective-permute-start.2) | collective-permute-done | bytes 3276832 | tf_op jit(solution)/shard_map/ppermute | solution.py:107
  210.7 9.1 %fusion.32 = bf16[512,640]{1,0:T(8,128)(2,1)S(1)} fusion(f32[512,640]{1,0:T(8,128)S(1)} %get-tuple-element.124, bf16[512,5120]{1,0:T(8,128)(2,1)S(1)} %get-tuple-element.115, bf16[2560,640]{1,0:T(8,128)(2,1)} %collective-permute-done.2, bf16[2560,640]{1,0:T(8,128)(2,1)} %maximum_select_fusion.2, pred[]{:T(512)S(6)} %eq.63, f32[640]{0:T(1024)S(1)} %convert_element_type.222), kind=kOutput, calls=%fused_computation.60 | convolution fusion | flops 3385917440 | bytes 13765121 | tf_op jit(solution)/shard_map/dot_general | solution.py:133
  221.0 14.8 %convert_reduce_fusion = (f32[5120]{0:T(1024)S(1)}, bf16[512,5120]{1,0:T(8,128)(2,1)}) fusion(f32[512,5120]{1,0:T(8,128)} %get-tuple-element.116, bf16[5120,640]{1,0:T(8,128)(2,1)} %all-gather.9.cloned.1.call-done, f32[512,640]{1,0:T(8,128)S(1)} %fusion.47, f32[512,5120]{1,0:T(8,128)} %get-tuple-element.125, f32[5120]{0:T(1024)S(1)} %bitcast.122), kind=kOutput, calls=%fused_computation.11 | convolution fusion | flops 3400330240 | bytes 34119680 | tf_op jit(solution)/shard_map/ld,fd->lf/dot_general | solution.py:163
  235.8 8.5 %multiply_reduce_fusion.1 = (f32[640]{0:T(1024)S(1)}, f32[512]{0:T(512)S(1)}, f32[640]{0:T(1024)S(1)}, f32[512,640]{1,0:T(8,128)S(1)}) fusion(f32[512,640]{1,0:T(8,128)S(1)} %copy-done.4, f32[512]{0:T(512)S(1)} %fusion.53, f32[512]{0:T(512)S(1)} %broadcast_multiply_fusion, f32[640]{0:T(1024)S(1)} %convert_element_type.217, ...), kind=kOutput, calls=%fused_computation.70 | convolution fusion | flops 3358063104 | bytes 14431744 | tf_op jit(solution)/shard_map/lf,df->ld/dot_general | solution.py:171
  252.0 13.9 %multiply_reduce_fusion = (f32[20,512]{1,0:T(8,128)S(1)}, f32[20,512,512]{1,2,0:T(8,128)}) fusion(f32[20,512,512]{1,2,0:T(8,128)} %copy-done.2, f32[20,512]{1,0:T(8,128)S(1)} %log_add_fusion, bf16[512,20,32]{0,2,1:T(8,128)(2,1)} %bitcast.110, bf16[512,3,20,32]{0,3,2,1:T(8,128)(2,1)S(1)} %bitcast.107), kind=kOutput, calls=%fused_computation.1 | convolution fusion | flops 351262720 | bytes 43343872 | tf_op jit(solution)/shard_map/while/body/eval_jaxpr/qhd,khd->hqk/dot_general | solution.py:209
  265.9 14.9 %multiply_convert_fusion = bf16[20,512,512]{1,2,0:T(8,128)(2,1)S(1)} fusion(f32[20,512,512]{1,2,0:T(8,128)} %get-tuple-element.130, f32[20,512,512]{1,2,0:T(8,128)} %copy-done.2, f32[20,512]{1,0:T(8,128)S(1)} %get-tuple-element.129, f32[20,512]{1,0:T(8,128)S(1)} %log_add_fusion), kind=kLoop, calls=%fused_computation | loop fusion | flops 20971520 | bytes 52510720 | tf_op jit(solution)/shard_map/while/body/eval_jaxpr/convert_element_type | solution.py:213
  285.6 9.1 %fusion.33 = bf16[20,32,512]{2,1,0:T(8,128)(2,1)S(1)} fusion(bf16[512,20,32]{0,2,1:T(8,128)(2,1)S(1)} %bitcast.111, f32[20,512,512]{1,2,0:T(8,128)} %copy-done.2, f32[20,512]{1,0:T(8,128)S(1)} %log_add_fusion), kind=kOutput, calls=%fused_computation.61 | convolution fusion | flops 346357760 | bytes 22323200 | tf_op jit(solution)/shard_map/while/body/eval_jaxpr/hqk,qhd->khd/dot_general | solution.py:203
  295.5 4.1 fusion.42
  301.0 12.3 %fusion.66 = f32[640,5120]{1,0:T(8,128)} fusion(bf16[512,5120]{1,0:T(8,128)(2,1)} %get-tuple-element.133, f32[512,640]{1,0:T(8,128)S(1)} %copy-done.5, f32[640]{0:T(1024)S(1)} %convert_element_type.218, f32[640]{0:T(1024)S(1)} %convert_element_type.217, f32[512]{0:T(512)S(1)} %fusion.53, f32[512]{0:T(512)S(1)} %broadcast_multiply_fusion), kind=kOutput, calls=%fused_computation.128 | convolution fusion | flops 3357081600 | bytes 19670016 | tf_op jit(solution)/shard_map/ld,lf->df/dot_general | solution.py:167
  313.3 12.1 %fusion.57 = f32[5120,640]{1,0:T(8,128)} fusion(bf16[512,5120]{1,0:T(8,128)(2,1)} %copy-done.11, f32[512,640]{1,0:T(8,128)S(1)} %fusion.47), kind=kOutput, calls=%fused_computation.122 | convolution fusion | flops 3355770880 | bytes 19660800 | tf_op jit(solution)/shard_map/lf,ld->fd/dot_general | solution.py:159
  327.4 27.5 %reduce-scatter.5.cloned.1.call-done = f32[80,1920]{1,0:T(8,128)} async-done(((f32[640,1920]{1,0:T(8,128)}), f32[80,1920]{1,0:T(8,128)}) %reduce-scatter.5.cloned.1.call-update) | async-done | bytes 614416 | tf_op jit(solution)/shard_map/reduce_scatter | solution.py:254
  356.7 96.4 %reduce-scatter.9.cloned.1.call-done = f32[80,5120]{1,0:T(8,128)} async-done(((f32[640,5120]{1,0:T(8,128)}), f32[80,5120]{1,0:T(8,128)}) %reduce-scatter.9.cloned.1.call-update) | async-done | bytes 1638416 | tf_op jit(solution)/shard_map/reduce_scatter | solution.py:177
  455.5 95.9 %reduce-scatter.11.cloned.1.call-done = f32[640,640]{1,0:T(8,128)} async-done(((f32[5120,640]{1,0:T(8,128)}), f32[640,640]{1,0:T(8,128)}) %reduce-scatter.11.cloned.1.call-update) | async-done | bytes 1638416 | tf_op jit(solution)/shard_map/reduce_scatter | solution.py:179
  556.7 4.0 fusion.68
  564.5 25.0 %all-reduce.19 = (bf16[640]{0:T(1024)(128)(2,1)S(1)}, bf16[640]{0:T(1024)(128)(2,1)S(1)}, bf16[640]{0:T(1024)(128)(2,1)S(1)}, bf16[640]{0:T(1024)(128)(2,1)S(1)}...) all-reduce(f32[640]{0:T(1024)S(1)} %get-tuple-element.70, ...), channel_id=2, replica_groups=mesh['narrow'=4,'wide'=8] {'wide'}, use_global_device_ids=true, to_apply=%region_14.15.clone | all-reduce | flops 10256 | bytes 61536
  592.6 12.5 %all-reduce.21 = (bf16[80]{0:T(256)(128)(2,1)S(1)}, bf16[80]{0:T(256)(128)(2,1)S(1)}, bf16[80]{0:T(256)(128)(2,1)S(1)}, bf16[80]{0:T(256)(128)(2,1)S(1)}, bf16[8...) all-reduce(bf16[80]{0:T(256)(128)(2,1)S(1)} %dynamic-slice.47, ...), channel_id=1, replica_groups=mesh['narrow'=4,'wide'=8] {'narrow'}, use_global_device_ids=true, to_apply=%region_15.16 | all-reduce | flops 1282 | bytes 5128 | tf_op jit(solution)/shard_map/psum | solution.py:261
  611.1 29.3 %all-reduce.25.cloned.1.call-done = (bf16[80,1920]{1,0:T(8,128)(2,1)}, bf16[80,640]{1,0:T(8,128)(2,1)}, bf16[80,5120]{1,0:T(8,128)(2,1)}, bf16[640,640]{1,0:T(8,128)(2,1)}) async-done(((bf16[80,1920]{1,0:T(8,128)(2,1)}, bf16[80,640]{1,0:T(8,128)(2,1)}, bf16[80,5120]{1,0:T(8,128)(2,1)}, bf16[640,640]{1,0:T(8,128)(2,1)}), (bf16[80,1920]{1,0:T(8,128)(2,1)}, bf16[80,640]{1,0:T(8,128)(2,1)}, ...) | async-done | bytes 2048016 | tf_op jit(solution)/shard_map/psum | solution.py:263
  (216 shorter events, 73.4 us)
Async XLA Ops:
  7.2 212.6 %copy-start = (bf16[640,25]{0,1:T(8,128)(2,1)S(1)}, bf16[640,25]{0,1:T(8,128)(2,1)}, u32[]{:S(2)}) copy-start(bf16[640,25]{0,1:T(8,128)(2,1)} %param.22) | copy-start | bytes 96004
  7.3 84.6 %copy-start.8 = (bf16[1,512,640]{2,1,0:T(8,128)(2,1)S(1)}, bf16[1,512,640]{2,1,0:T(8,128)(2,1)}, u32[]{:S(2)}) copy-start(bf16[1,512,640]{2,1,0:T(8,128)(2,1)} %param.18) | copy-start | bytes 1966084
  7.3 85.1 %copy-start.25 = (bf16[80,640]{1,0:T(8,128)(2,1)S(1)}, bf16[80,640]{1,0:T(8,128)(2,1)}, u32[]{:S(2)}) copy-start(bf16[80,640]{1,0:T(8,128)(2,1)} %param.28) | copy-start | bytes 307204
  7.3 97.9 %copy-start.34 = (s32[1,512]{1,0:T(1,128)S(1)}, s32[1,512]{1,0:T(1,128)}, u32[]{:S(2)}) copy-start(s32[1,512]{1,0:T(1,128)} %param.19) | copy-start | bytes 6148
  7.4 104.5 %all-gather.5.cloned.1.call-start = ((), (), s32[]{:S(2)}) async-start(), calls=%async_computation.4 | async-start | bytes 2764800 | tf_op jit(solution)/shard_map/all_gather | solution.py:61
  8.1 127.5 %all-gather.7.cloned.1.call-start = ((), (), s32[]{:S(2)}) async-start(), calls=%async_computation.5 | async-start | bytes 7372800 | tf_op jit(solution)/shard_map/all_gather | solution.py:117
  8.8 212.2 %all-gather.9.cloned.1.call-start = ((), (), s32[]{:S(2)}) async-start(), calls=%async_computation.6 | async-start | bytes 7372800 | tf_op jit(solution)/shard_map/all_gather | solution.py:156
  8.9 2.7 collective-permute-start
  13.6 92.6 %collective-permute-start.1 = (bf16[1280,640]{1,0:T(8,128)(2,1)S(1)}, bf16[1280,640]{1,0:T(8,128)(2,1)}, u32[]{:S(2)}, u32[]{:S(2)}) collective-permute-start(bf16[1280,640]{1,0:T(8,128)(2,1)S(1)} %maximum_select_fusion.3), channel_id=1, source_target_pairs={{0,2},{1,3},{2,0},{3,1},{4,6},{5,7},{6,4},{7,5},{8,10},{9,11},{10,... | collective-permute-start | bytes 4915208 | tf_op jit(solution)/shard_map/ppermute | solution.py:107
  16.5 309.2 %reduce-scatter.7.cloned.1.call-start = ((), (), s32[]{:S(2)}) async-start(), calls=%async_computation.8 | async-start | bytes 1843200 | tf_op jit(solution)/shard_map/reduce_scatter | solution.py:257
  82.3 29.6 %copy-start.26 = (f32[640]{0:T(1024)}, f32[640]{0:T(1024)S(1)}, u32[]{:S(2)}) copy-start(f32[640]{0:T(1024)S(1)} %convert_element_type.208) | copy-start | bytes 7684
  82.3 29.6 %copy-start.38 = (f32[640]{0:T(1024)}, f32[640]{0:T(1024)S(1)}, u32[]{:S(2)}) copy-start(f32[640]{0:T(1024)S(1)} %convert_element_type.209) | copy-start | bytes 7684
  92.4 24.6 %copy-start.30 = (f32[512]{0:T(512)}, f32[512]{0:T(512)S(1)}, u32[]{:S(2)}) copy-start(f32[512]{0:T(512)S(1)} %fusion.40) | copy-start | bytes 6148
  110.8 99.8 %collective-permute-start.2 = (bf16[2560,640]{1,0:T(8,128)(2,1)}, bf16[2560,640]{1,0:T(8,128)(2,1)}, u32[]{:S(2)}, u32[]{:S(2)}) collective-permute-start(bf16[2560,640]{1,0:T(8,128)(2,1)} %maximum_select_fusion.2), channel_id=1, source_target_pairs={{0,4},{1,5},{2,6},{3,7},{4,0},{5,1},{6,2},{7,3},{8,12},{9,13},{10,... | collective-permute-start | bytes 9830408 | tf_op jit(solution)/shard_map/ppermute | solution.py:107
  135.3 75.4 %copy-start.3 = (f32[512,640]{1,0:T(8,128)}, f32[512,640]{1,0:T(8,128)S(1)}, u32[]{:S(2)}) copy-start(f32[512,640]{1,0:T(8,128)S(1)} %get-tuple-element.124) | copy-start | bytes 3932164
  166.3 53.5 %copy-start.11 = (bf16[512,5120]{1,0:T(8,128)(2,1)}, bf16[512,5120]{1,0:T(8,128)(2,1)S(1)}, u32[]{:S(2)}) copy-start(bf16[512,5120]{1,0:T(8,128)(2,1)S(1)} %get-tuple-element.115) | copy-start | bytes 15728644
  252.0 102.8 %reduce-scatter.5.cloned.1.call-start = ((), (), s32[]{:S(2)}) async-start(), calls=%async_computation.7 | async-start | bytes 5529600 | tf_op jit(solution)/shard_map/reduce_scatter | solution.py:254
  299.7 153.4 %reduce-scatter.9.cloned.1.call-start = ((), (), s32[]{:S(2)}) async-start(), calls=%async_computation.9 | async-start | bytes 14745600 | tf_op jit(solution)/shard_map/reduce_scatter | solution.py:177
  313.2 238.2 %reduce-scatter.11.cloned.1.call-start = ((), (), s32[]{:S(2)}) async-start(), calls=%async_computation.10 | async-start | bytes 14745600 | tf_op jit(solution)/shard_map/reduce_scatter | solution.py:179
  325.4 314.9 %all-reduce.25.cloned.1.call-start = ((), (), s32[]{:S(2)}) async-start(), calls=%async_computation.11 | async-start | bytes 4096000 | tf_op jit(solution)/shard_map/psum | solution.py:263
  327.4 227.8 %copy-start.37 = (s32[1,512]{1,0:T(1,128)S(1)}, s32[1,512]{1,0:T(1,128)}, u32[]{:S(2)}) copy-start(s32[1,512]{1,0:T(1,128)} %param.21) | copy-start | bytes 6148
  327.4 229.0 %copy-start.14 = (bf16[20,32,512]{2,1,0:T(8,128)(2,1)S(1)}, bf16[20,32,512]{2,1,0:T(8,128)(2,1)}, u32[]{:S(2)}) copy-start(bf16[20,32,512]{2,1,0:T(8,128)(2,1)} %copy-done.13) | copy-start | bytes 1966084
  327.4 229.0 %copy-start.16 = (bf16[20,32,512]{2,1,0:T(8,128)(2,1)S(1)}, bf16[20,32,512]{2,1,0:T(8,128)(2,1)}, u32[]{:S(2)}) copy-start(bf16[20,32,512]{2,1,0:T(8,128)(2,1)} %copy-done.15) | copy-start | bytes 1966084
  561.5 86.1 %copy-start.1 = (bf16[640,25]{0,1:T(8,128)(2,1)S(1)}, bf16[640,25]{0,1:T(8,128)(2,1)}, u32[]{:S(2)}) copy-start(bf16[640,25]{0,1:T(8,128)(2,1)} %param.22) | copy-start | bytes 96004
  (37 other events, 288.7 us)
Sparse Core Ops, SparseCore 0:
  10.0 41.9 all-gather.4
  53.9 47.8 all-gather.6
  103.7 73.1 all-gather.8
  252.1 38.8 reduce-scatter.6
  299.8 55.0 reduce-scatter.4
  358.3 94.7 reduce-scatter.8
  456.6 94.7 reduce-scatter.10
  555.2 85.1 all-reduce.24
